TPU v7x, 32 devices: a whole 2x2x4 slice. The times are simulated.
32 devices in a mesh: row: 8 (over z, y), col: 4 (over x, core).
Axes of the slice: x: 2, y: 2, z: 4, core: 2. Of those that a mesh axis runs over, the one named last changes fastest.
Arguments:
- queries: bfloat16 [1024, 1024], P('row', 'col'), may hold values from -26 to 26
- key_vectors: bfloat16 [1024, 1024], P('row', 'col'), may hold values from -8 to 8
- values: bfloat16 [1024, 1024], P('row', 'col'), may hold values from -6 to 6
- sink_logit: float32 [8], P('col'), may hold values from -1 to 5
- lengths: int32 [8], replicated, may hold values from 1 to 576, as said below
- stream: bfloat16 [1024, 2048], P('row', 'col'), may hold values from -60 to 60
- out_weight: bfloat16 [1024, 2048], P('col', 'row'), may hold values from -0.1875 to 0.1875
- norm_gain: bfloat16 [2048], P('col'), may hold values from 0.25 to 1.75
- shared_gate: bfloat16 [2048, 2816], P('row', 'col'), may hold values from -0.125 to 0.125
- shared_up: bfloat16 [2048, 2816], P('row', 'col'), may hold values from -0.125 to 0.125
- shared_down: bfloat16 [2816, 2048], P('col', 'row'), may hold values from -0.109375 to 0.109375
- shared_switch: bfloat16 [2048], replicated, may hold values from -0.125 to 0.125
- expert_gate: bfloat16 [8, 2048, 1408], P('row', None, 'col'), may hold values from -0.125 to 0.125
- expert_up: bfloat16 [8, 2048, 1408], P('row', None, 'col'), may hold values from -0.125 to 0.125
- expert_down: bfloat16 [8, 1408, 2048], P('row', 'col'), may hold values from -0.15625 to 0.15625
- routes: int32 [1024, 4], P('row'), may hold values from 0 to 7, all different within a row; in each aligned block of 128 rows (0 to 127, 128 to 255, ...) at most 96 rows name the same one
- route_weights: float32 [1024, 4], P('row'), may hold values from 0.05 to 0.6
Outputs:
- attended: bfloat16 [1024, 1024], P('row', 'col')
- layer_out: bfloat16 [1024, 2048], P('row', 'col')
Inputs may be any that keep to these rules, and one draw needn't show every extreme that they name: `routes`: each row names 4 different experts; among the 128 rows of one device (aligned blocks) no expert is named more than 96 times, a bound that some block reaches. The lengths sum to 1024; exactly one prompt has 576 tokens.
All inputs are finite; a program needn't handle non-finite values.
Results may differ from a plain program's by a relative error of at most 0.01.
Values may be sent and summed in bfloat16 or wider, within the bound.
A program may use at most 128 MiB of HBM per device.

v0:
```python
import math
import jax
import jax.numpy as jnp
from jax import lax
from jax.sharding import PartitionSpec as P

HDIM = 128
WINDOW = 4096
norm_eps = 1e-06
masked_score = -1e30


def lower_bounds(lengths, positions):
    doc_ends = jnp.cumsum(lengths)
    starts = doc_ends - lengths
    begun_docs = starts[None, :] <= positions[:, None]
    doc_start = jnp.max(jnp.where(begun_docs, starts[None, :], 0), axis=1)
    return jnp.maximum(doc_start, positions - WINDOW + 1)


def body(
    queries,
    key_vectors,
    values,
    sink_logit,
    lengths,
    stream,
    out_weight,
    norm_gain,
    shared_gate,
    shared_up,
    shared_down,
    shared_switch,
    expert_gate,
    expert_up,
    expert_down,
    routes,
    route_weights,
):
    local_tokens = queries.shape[0]
    feature_width = queries.shape[1]
    head_count = feature_width // HDIM
    my_row = lax.axis_index("row")
    positions = my_row * local_tokens + jnp.arange(local_tokens, dtype=jnp.int32)
    lower_bound = lower_bounds(lengths, positions)
    query_heads = queries.reshape(local_tokens, head_count, HDIM)
    score_scale = 1.0 / math.sqrt(HDIM)
    key_value = jnp.stack([key_vectors, values], 0)
    key_piece = lax.all_gather(key_value, "row", axis=1, tiled=True)
    row_max = jnp.broadcast_to(sink_logit[None, :], (local_tokens, head_count))
    denominator = jnp.ones((local_tokens, head_count), jnp.float32)
    numerator = jnp.zeros((local_tokens, head_count, HDIM), jnp.float32)
    needed = key_piece.shape[1]
    key_heads = key_piece[0].reshape(needed, head_count, HDIM)
    value_heads = key_piece[1].reshape(needed, head_count, HDIM)
    scores = (
        jnp.einsum("qhd,khd->qhk", query_heads, key_heads, preferred_element_type=jnp.float32)
        * score_scale
    )
    key_places = jnp.arange(needed, dtype=jnp.int32)
    visible = (
        (key_places[None, :] >= lower_bound[:, None]) & (key_places[None, :] <= positions[:, None])
    )[:, None, :]
    masked = jnp.where(visible, scores, masked_score)
    new_max = jnp.maximum(row_max, jnp.max(masked, axis=2))
    weight = jnp.where(visible, jnp.exp(masked - new_max[:, :, None]), 0.0)
    rescale = jnp.exp(row_max - new_max)
    denominator = denominator * rescale + jnp.sum(weight, axis=2)
    numerator = numerator * rescale[:, :, None] + jnp.einsum(
        "qhk,khd->qhd", weight.astype(jnp.bfloat16), value_heads, preferred_element_type=jnp.float32
    )
    final_max, denominator, numerator = (new_max, denominator, numerator)
    attended = (
        (numerator / denominator[:, :, None])
        .reshape(local_tokens, feature_width)
        .astype(jnp.bfloat16)
    )
    head_terms = jnp.dot(
        attended,
        lax.all_gather(out_weight, "row", axis=1, tiled=True),
        preferred_element_type=jnp.float32,
    )
    mixed_heads = lax.psum_scatter(
        head_terms.astype(jnp.bfloat16), "col", scatter_dimension=1, tiled=True
    ).astype(jnp.float32)
    hidden = (stream.astype(jnp.float32) + mixed_heads).astype(jnp.bfloat16)
    widened = hidden.astype(jnp.float32)
    full_width = lax.axis_size("col") * hidden.shape[1]
    squares = lax.psum(jnp.sum(widened * widened, axis=1), "col")
    row_scale = lax.rsqrt(squares / full_width + norm_eps)
    normed_part = (widened * row_scale[:, None] * norm_gain.astype(jnp.float32)).astype(
        jnp.bfloat16
    )
    normed = lax.all_gather(normed_part, "col", axis=1, tiled=True)
    gate_part = jnp.dot(
        normed,
        lax.all_gather(shared_gate, "row", axis=0, tiled=True),
        preferred_element_type=jnp.float32,
    )
    up_part = jnp.dot(
        normed,
        lax.all_gather(shared_up, "row", axis=0, tiled=True),
        preferred_element_type=jnp.float32,
    )
    shared_act = (jax.nn.silu(gate_part) * up_part).astype(jnp.bfloat16)
    shared_part = jnp.dot(
        shared_act,
        lax.all_gather(shared_down, "row", axis=1, tiled=True),
        preferred_element_type=jnp.float32,
    )
    switch = jax.nn.sigmoid(jnp.dot(normed, shared_switch, preferred_element_type=jnp.float32))
    row_count = lax.axis_size("row")
    fanout = routes.shape[1]
    model_width = normed.shape[1]
    capacity = max(2, min(local_tokens, 3 * local_tokens * fanout // (2 * row_count)))
    flat_routes = routes.reshape(-1)
    onehot = (flat_routes[:, None] == jnp.arange(row_count, dtype=jnp.int32)[None, :]).astype(
        jnp.int32
    )
    before = jnp.cumsum(onehot, axis=0) - onehot
    slot_index = jnp.sum(before * onehot, axis=1)
    target = flat_routes * capacity + slot_index
    owner_row = jnp.arange(local_tokens * fanout, dtype=jnp.int32) // fanout
    source = jnp.full((row_count * capacity,), local_tokens, jnp.int32).at[target].set(owner_row)
    padded = jnp.concatenate([normed, jnp.zeros((1, model_width), jnp.bfloat16)], 0)
    outgoing = padded[source].reshape(row_count, capacity, model_width)
    received = lax.all_to_all(outgoing, "row", split_axis=0, concat_axis=0, tiled=True)
    senders, slot_count, received_width = received.shape
    dispatched = received.reshape(senders * slot_count, received_width)
    gate_out = jnp.dot(dispatched, expert_gate[0], preferred_element_type=jnp.float32)
    up_out = jnp.dot(dispatched, expert_up[0], preferred_element_type=jnp.float32)
    activation = (jax.nn.silu(gate_out) * up_out).astype(jnp.bfloat16)
    partial_out = jnp.dot(activation, expert_down[0], preferred_element_type=jnp.float32).astype(
        jnp.bfloat16
    )
    returned = lax.all_to_all(
        partial_out.reshape(senders, slot_count, received_width),
        "row",
        split_axis=0,
        concat_axis=0,
        tiled=True,
    )
    route_rows = returned.reshape(row_count * capacity, model_width)[target].reshape(
        local_tokens, fanout, model_width
    )
    routed = jnp.zeros((local_tokens, model_width), jnp.float32)
    for route_slot in range(fanout):
        routed = routed + route_weights[:, route_slot][:, None] * route_rows[
            :, route_slot, :
        ].astype(jnp.float32)
    layer_terms = switch[:, None] * shared_part + routed
    summed = lax.psum_scatter(
        layer_terms.astype(jnp.bfloat16), "col", scatter_dimension=1, tiled=True
    ).astype(jnp.float32)
    layer_out = (hidden.astype(jnp.float32) + summed).astype(jnp.bfloat16)
    return (attended, layer_out)


def solution(mesh):
    return jax.shard_map(
        body,
        mesh=mesh,
        in_specs=(
            P("row", "col"),
            P("row", "col"),
            P("row", "col"),
            P("col"),
            P(),
            P("row", "col"),
            P("col", "row"),
            P("col"),
            P("row", "col"),
            P("row", "col"),
            P("col", "row"),
            P(),
            P("row", None, "col"),
            P("row", None, "col"),
            P("row", "col", None),
            P("row", None),
            P("row", None),
        ),
        out_specs=(P("row", "col"), P("row", "col")),
        check_vma=False,
    )
```

profile of v0, /device:TPU:0, one launch (start us, length us, event | category | flops | bytes accessed | tf_op | source)
XLA Modules:
  0.0 430.8 jit_solution(6506192966484894538)
XLA Ops:
  12.5 40.4 %all-gather.6.cloned.1.call-done = bf16[2,1024,256]{1,2,0:T(8,128)(2,1)} async-done(((bf16[2,128,256]{1,2,0:T(8,128)(2,1)}), bf16[2,1024,256]{1,2,0:T(8,128)(2,1)}) %all-gather.6.cloned.1.call-update) | async-done | bytes 1048592 | tf_op jit(solution)/shard_map/all_gather | solution.py:49
  52.9 1.3 fusion.62
  55.4 38.0 %all-gather.8.cloned.1.call-done = bf16[256,2048]{1,0:T(8,128)(2,1)} async-done(((bf16[256,256]{1,0:T(8,128)(2,1)}), bf16[256,2048]{1,0:T(8,128)(2,1)}) %all-gather.8.cloned.1.call-update) | async-done | bytes 1048592 | tf_op jit(solution)/shard_map/all_gather | solution.py:80
  93.4 2.4 convolution_convert_fusion.1
  96.8 1.1 reduce-window.20
  98.5 2.4 scatter_custom_fusion
  101.0 15.5 %reduce-scatter.3.cloned.1.call-done = bf16[128,512]{1,0:T(8,128)(2,1)} async-done(((bf16[128,2048]{1,0:T(8,128)(2,1)}), bf16[128,512]{1,0:T(8,128)(2,1)}) %reduce-scatter.3.cloned.1.call-update) | async-done | bytes 131088 | tf_op jit(solution)/shard_map/reduce_scatter | solution.py:83
  117.5 5.8 %psum.7 = f32[128]{0:T(128)S(1)} all-reduce(f32[128]{0:T(128)S(1)} %fusion.41), channel_id=1, replica_groups=mesh['row'=8,'col'=4] {'col'}, use_global_device_ids=true, to_apply=%region_6.7 | all-reduce | flops 128 | bytes 1024 | tf_op jit(solution)/shard_map/psum | solution.py:89
  124.3 7.3 %all_gather.20 = bf16[128,2048]{1,0:T(8,128)(2,1)S(1)} all-gather(bf16[128,512]{1,0:T(8,128)(2,1)S(1)} %fusion.43), channel_id=1, replica_groups=mesh['row'=8,'col'=4] {'col'}, dimensions={1}, use_global_device_ids=true | all-gather | bytes 655360 | tf_op jit(solution)/shard_map/all_gather | solution.py:94
  131.7 4.3 gather_fusion
  135.9 5.5 %all-to-all-start = ((bf16[8,96,2048]{2,1,0:T(8,128)(2,1)}), bf16[8,96,2048]{2,1,0:T(8,128)(2,1)}, u32[]{:S(2)}, u32[]{:S(2)}) async-start(bf16[8,96,2048]{2,1,0:T(8,128)(2,1)} %bitcast.109), calls=%async_computation.1 | async-start | bytes 6291456 | tf_op jit(solution)/shard_map/all_to_all | solution.py:127
  142.1 94.2 %all-to-all-done = bf16[8,96,2048]{2,1,0:T(8,128)(2,1)} async-done(((bf16[8,96,2048]{2,1,0:T(8,128)(2,1)}), bf16[8,96,2048]{2,1,0:T(8,128)(2,1)}, u32[]{:S(2)}, u32[]{:S(2)}) %all-to-all-start) | async-done | bytes 3145760 | tf_op jit(solution)/shard_map/all_to_all | solution.py:127
  236.2 4.7 %fusion.5 = f32[768,352]{0,1:T(8,128)} fusion(bf16[768,2048]{1,0:T(8,128)(2,1)} %bitcast.16, bf16[1,2048,352]{1,2,0:T(8,128)(2,1)} %param.29), kind=kOutput, calls=%fused_computation.11 | convolution fusion | flops 1107296256 | bytes 5668864 | tf_op jit(solution)/shard_map/dot_general | solution.py:130
  240.9 8.0 %convolution_convert_fusion = bf16[768,2048]{1,0:T(8,128)(2,1)} fusion(bf16[1,352,2048]{2,1,0:T(8,128)(2,1)S(1)} %copy-done, bf16[768,2048]{1,0:T(8,128)(2,1)} %bitcast.16, bf16[1,2048,352]{1,2,0:T(8,128)(2,1)} %param.30, f32[768,352]{0,1:T(8,128)} %fusion.5), kind=kOutput, calls=%fused_computation.3 | convolution fusion | flops 2217787392 | bytes 10256384 | tf_op jit(solution)/shard_map/dot_general | solution.py:133
  248.9 4.6 %all-to-all-start.1 = ((bf16[8,96,2048]{2,1,0:T(8,128)(2,1)}), bf16[8,96,2048]{2,1,0:T(8,128)(2,1)}, u32[]{:S(2)}, u32[]{:S(2)}) async-start(bf16[8,96,2048]{2,1,0:T(8,128)(2,1)} %bitcast.110), calls=%async_computation.2 | async-start | bytes 6291456 | tf_op jit(solution)/shard_map/all_to_all | solution.py:136
  255.1 3.5 fusion.64
  258.6 92.9 %all-to-all-done.1 = bf16[8,96,2048]{2,1,0:T(8,128)(2,1)} async-done(((bf16[8,96,2048]{2,1,0:T(8,128)(2,1)}), bf16[8,96,2048]{2,1,0:T(8,128)(2,1)}, u32[]{:S(2)}, u32[]{:S(2)}) %all-to-all-start.1) | async-done | bytes 3145760 | tf_op jit(solution)/shard_map/all_to_all | solution.py:136
  351.5 7.5 %gather_fusion.1 = bf16[512,2048]{1,0:T(8,128)(2,1)} fusion(bf16[768,2048]{1,0:T(8,128)(2,1)} %bitcast.21, s32[1024]{0:T(1024)S(1)} %pad_clamp_fusion), kind=kCustom, calls=%fused_computation.1 | custom fusion | bytes 4196352 | tf_op jit(solution)/shard_map/gather | solution.py:143
  359.0 2.7 reshape.220
  361.8 4.5 %fusion.61 = (bf16[128,1,2048]{2,1,0:T(2,128)(2,1)}, bf16[128,1,2048]{2,1,0:T(2,128)(2,1)}, bf16[128,1,2048]{2,1,0:T(2,128)(2,1)}, bf16[128,1,2048]{2,1,0:T(2,128)(2,1)}) fusion(bf16[128,4,2048]{2,1,0:T(4,128)(2,1)S(1)} %reshape.220), kind=kLoop, calls=%fused_computation.104 | loop fusion | bytes 4194304 | tf_op jit(solution)/shard_map/slice | solution.py:148
  366.3 27.9 %all-gather.14.cloned.1.call-done = bf16[704,2048]{1,0:T(8,128)(2,1)} async-done(((bf16[704,256]{1,0:T(8,128)(2,1)}), bf16[704,2048]{1,0:T(8,128)(2,1)}) %all-gather.14.cloned.1.call-update) | async-done | bytes 2883600 | tf_op jit(solution)/shard_map/all_gather | solution.py:108
  394.2 8.1 %fusion.1 = bf16[128,2048]{1,0:T(8,128)(2,1)} fusion(bf16[704,2048]{1,0:T(8,128)(2,1)} %all-gather.14.cloned.1.call-done, bf16[128,2048]{1,0:T(8,128)(2,1)} %copy-done.1, bf16[2048,704]{0,1:T(8,128)(2,1)} %all-gather.12.cloned.1.call-done, bf16[128,1,2048]{2,1,0:T(2,128)(2,1)} %get-tuple-element.11, bf16[128,1,2048]{2,1,0:T(2,128)(2,1)} %get-tuple-element.9, ...), kind=kOutput, calls=%fused_computation.6 | convolution fusion | flops 742408192 | bytes 9275904 | tf_op jit(solution)/shard_map/dot_general | solution.py:106
  403.1 19.3 %reduce-scatter.5.cloned.1.call-done = bf16[128,512]{1,0:T(8,128)(2,1)} async-done(((bf16[128,2048]{1,0:T(8,128)(2,1)}), bf16[128,512]{1,0:T(8,128)(2,1)}) %reduce-scatter.5.cloned.1.call-update) | async-done | bytes 131088 | tf_op jit(solution)/shard_map/reduce_scatter | solution.py:152
  422.3 1.6 fusion.44
  (81 shorter events, 12.9 us)
Async XLA Ops:
  7.2 233.7 %copy-start = (bf16[1,352,2048]{2,1,0:T(8,128)(2,1)S(1)}, bf16[1,352,2048]{2,1,0:T(8,128)(2,1)}, u32[]{:S(2)}) copy-start(bf16[1,352,2048]{2,1,0:T(8,128)(2,1)} %param.31) | copy-start | bytes 4325380
  7.2 47.0 %copy-start.7 = (bf16[128,256]{1,0:T(8,128)(2,1)S(1)}, bf16[128,256]{1,0:T(8,128)(2,1)}, u32[]{:S(2)}) copy-start(bf16[128,256]{1,0:T(8,128)(2,1)} %param.17) | copy-start | bytes 196612
  7.2 45.7 %all-gather.6.cloned.1.call-start = ((), (), s32[]{:S(2)}) async-start(), calls=%async_computation.4 | async-start | bytes 1179648 | tf_op jit(solution)/shard_map/all_gather | solution.py:49
  10.0 44.6 %copy-start.10 = (f32[2]{0:T(128)S(1)}, f32[2]{0:T(128)}, u32[]{:S(2)}) copy-start(f32[2]{0:T(128)} %param.20) | copy-start | bytes 28
  10.0 83.4 %all-gather.8.cloned.1.call-start = ((), (), s32[]{:S(2)}) async-start(), calls=%async_computation.5 | async-start | bytes 1179648 | tf_op jit(solution)/shard_map/all_gather | solution.py:80
  10.7 105.8 %reduce-scatter.3.cloned.1.call-start = ((), (), s32[]{:S(2)}) async-start(), calls=%async_computation.6 | async-start | bytes 655360 | tf_op jit(solution)/shard_map/reduce_scatter | solution.py:83
  54.9 41.4 %copy-start.8 = (s32[128,4]{0,1:T(4,128)S(1)}, s32[128,4]{0,1:T(4,128)}, u32[]{:S(2)}) copy-start(s32[128,4]{0,1:T(4,128)} %param.32) | copy-start | bytes 6148
  54.9 41.8 %copy-start.12 = (bf16[512]{0:T(512)(128)(2,1)S(1)}, bf16[512]{0:T(512)(128)(2,1)}, u32[]{:S(2)}) copy-start(bf16[512]{0:T(512)(128)(2,1)} %param.24) | copy-start | bytes 3076
  55.3 40.5 %copy-start.5 = (bf16[128,2,128]{0,2,1:T(8,128)(2,1)}, bf16[128,2,128]{0,2,1:T(8,128)(2,1)S(1)}, u32[]{:S(2)}) copy-start(bf16[128,2,128]{0,2,1:T(8,128)(2,1)S(1)} %fusion.18) | copy-start | bytes 196612
  55.4 61.1 %copy-start.2 = (bf16[128,512]{1,0:T(8,128)(2,1)S(1)}, bf16[128,512]{1,0:T(8,128)(2,1)}, u32[]{:S(2)}) copy-start(bf16[128,512]{1,0:T(8,128)(2,1)} %param.22) | copy-start | bytes 393220
  95.8 159.3 %all-gather.10.cloned.1.call-start = ((), (), s32[]{:S(2)}) async-start(), calls=%async_computation.7 | async-start | bytes 3244032 | tf_op jit(solution)/shard_map/all_gather | solution.py:97
  131.6 123.5 %copy-start.1 = (bf16[128,2048]{1,0:T(8,128)(2,1)}, bf16[128,2048]{1,0:T(8,128)(2,1)S(1)}, u32[]{:S(2)}) copy-start(bf16[128,2048]{1,0:T(8,128)(2,1)S(1)} %all_gather.20) | copy-start | bytes 1572868
  135.9 100.3 %all-to-all-start = ((bf16[8,96,2048]{2,1,0:T(8,128)(2,1)}), bf16[8,96,2048]{2,1,0:T(8,128)(2,1)}, u32[]{:S(2)}, u32[]{:S(2)}) async-start(bf16[8,96,2048]{2,1,0:T(8,128)(2,1)} %bitcast.109), calls=%async_computation.1 | async-start | bytes 6291456 | tf_op jit(solution)/shard_map/all_to_all | solution.py:127
  141.5 224.8 %all-gather.12.cloned.1.call-start = ((), (), s32[]{:S(2)}) async-start(), calls=%async_computation.8 | async-start | bytes 3244032 | tf_op jit(solution)/shard_map/all_gather | solution.py:102
  248.9 5.4 %copy-start.9 = (bf16[2048]{0:T(1024)(128)(2,1)S(1)}, bf16[2048]{0:T(1024)(128)(2,1)}, u32[]{:S(2)}) copy-start(bf16[2048]{0:T(1024)(128)(2,1)} %param.28) | copy-start | bytes 12292
  248.9 5.4 %copy-start.11 = (f32[128,4]{0,1:T(4,128)S(1)}, f32[128,4]{0,1:T(4,128)}, u32[]{:S(2)}) copy-start(f32[128,4]{0,1:T(4,128)} %param.33) | copy-start | bytes 6148
  248.9 102.6 %all-to-all-start.1 = ((bf16[8,96,2048]{2,1,0:T(8,128)(2,1)}), bf16[8,96,2048]{2,1,0:T(8,128)(2,1)}, u32[]{:S(2)}, u32[]{:S(2)}) async-start(bf16[8,96,2048]{2,1,0:T(8,128)(2,1)} %bitcast.110), calls=%async_computation.2 | async-start | bytes 6291456 | tf_op jit(solution)/shard_map/all_to_all | solution.py:136
  253.5 140.7 %all-gather.14.cloned.1.call-start = ((), (), s32[]{:S(2)}) async-start(), calls=%async_computation.9 | async-start | bytes 3244032 | tf_op jit(solution)/shard_map/all_gather | solution.py:108
  254.1 168.3 %reduce-scatter.5.cloned.1.call-start = ((), (), s32[]{:S(2)}) async-start(), calls=%async_computation.10 | async-start | bytes 655360 | tf_op jit(solution)/shard_map/reduce_scatter | solution.py:152
  394.2 8.1 %copy-start.6 = (bf16[128,2,128]{0,2,1:T(8,128)(2,1)S(1)}, bf16[128,2,128]{0,2,1:T(8,128)(2,1)}, u32[]{:S(2)}) copy-start(bf16[128,2,128]{0,2,1:T(8,128)(2,1)} %copy-done.5) | copy-start | bytes 196612
  394.2 28.1 %copy-start.3 = (bf16[128,512]{1,0:T(8,128)(2,1)S(1)}, bf16[128,512]{1,0:T(8,128)(2,1)}, u32[]{:S(2)}) copy-start(bf16[128,512]{1,0:T(8,128)(2,1)} %param.22) | copy-start | bytes 393220
  394.2 28.1 %copy-start.4 = (bf16[128,512]{1,0:T(8,128)(2,1)S(1)}, bf16[128,512]{1,0:T(8,128)(2,1)}, u32[]{:S(2)}) copy-start(bf16[128,512]{1,0:T(8,128)(2,1)} %reduce-scatter.3.cloned.1.call-done) | copy-start | bytes 393220
Sparse Core Ops, SparseCore 0:
  10.6 42.2 all-gather.5
  55.0 38.4 all-gather.7
  95.9 20.5 reduce-scatter.2
  118.6 109.6 all-gather.9
  230.3 102.7 all-gather.11
  335.3 58.9 all-gather.13
  402.4 19.8 reduce-scatter.4
where the time goes:
time: 431 us
  waiting for transfers between devices  330 us (77%)
  matrix products  27.7 us (6%)
  local copies, waits for them, and re-layouts  26.9 us (6%)
  between operations  14.4 us (3%)
  blocking collectives  13.1 us (3%)
  starting transfers between devices  10.6 us (2%)
  other arithmetic  7.72 us (2%)
    all_to_all x1, waiting for transfers between devices, body(): lax.all_to_all(outgoing, 'row', split_axis=0, concat_axis=0, tiled=True)  94.2 us
    all_to_all x1, waiting for transfers between devices, body(): lax.all_to_all(partial_out.reshape(senders, slot_count, received_width),...  92.9 us
    all_gather x1, waiting for transfers between devices, body(): key_piece = lax.all_gather(key_value, 'row', axis=1, tiled=True)  40.4 us
    all_gather x1, waiting for transfers between devices, body(): lax.all_gather(out_weight, 'row', axis=1, tiled=True)  38 us
    all_gather x1, waiting for transfers between devices, body(): lax.all_gather(shared_down, 'row', axis=1, tiled=True)  27.9 us
    reduce_scatter x1, waiting for transfers between devices, body(): lax.psum_scatter(layer_terms.astype(jnp.bfloat16), 'col', scatter_dimensi...  19.3 us
    reduce_scatter x1, waiting for transfers between devices, body(): lax.psum_scatter(head_terms.astype(jnp.bfloat16), 'col', scatter_dimensio...  15.5 us
  transfers between devices with their start and end apart: 9, of which 7 were waited for; matrix products, arithmetic and copies ran while one was open for 11% of the time, Pallas kernels for 0%

commit v1 on v0

--- a/solution.py
+++ b/solution.py
@@ -46,7 +46,12 @@
     query_heads = queries.reshape(local_tokens, head_count, HDIM)
     score_scale = 1.0 / math.sqrt(HDIM)
     key_value = jnp.stack([key_vectors, values], 0)
-    key_piece = lax.all_gather(key_value, "row", axis=1, tiled=True)
+    ring = [key_value]
+    for hop in range(7):
+        ring.append(lax.ppermute(ring[-1], "row", [(dev, (dev + 1) % 8) for dev in range(8)]))
+    key_piece = jnp.roll(
+        jnp.concatenate(ring[::-1], axis=1), (lax.axis_index("row") + 1) * ring[0].shape[1], axis=1
+    )
     row_max = jnp.broadcast_to(sink_logit[None, :], (local_tokens, head_count))
     denominator = jnp.ones((local_tokens, head_count), jnp.float32)
     numerator = jnp.zeros((local_tokens, head_count, HDIM), jnp.float32)

time: 431 us -> 410 us (0.951)
  waiting for transfers between devices: 330 us -> 306 us
    ppermute x0 -> x7, waiting for transfers between devices: none -> 54.2 us  [body(): lax.ppermute(ring[-1], 'row', [(dev, (dev + 1) % 8) for dev in range(8)])]
    all_gather x1 -> x0, waiting for transfers between devices: 40.4 us -> none  [body(): key_piece = lax.all_gather(key_value, 'row', axis=1, tiled=True)]
    all_gather x1, waiting for transfers between devices: 38 us -> 0.02 us  [body(): lax.all_gather(out_weight, 'row', axis=1, tiled=True)]
    all_gather x1, waiting for transfers between devices: 27.9 us -> 0.01 us  [body(): lax.all_gather(shared_down, 'row', axis=1, tiled=True)]
    all_gather x1, waiting for transfers between devices: 0.01 us -> 27.7 us  [body(): lax.all_gather(shared_up, 'row', axis=0, tiled=True)]
  transfers between devices with their start and end apart: 9 -> 15, of which waited for: 7 -> 12; matrix products, arithmetic and copies ran while one was open for 11% -> 11% of each run, Pallas kernels for 0% -> 0%
where the time goes in v1:
time: 410 us; the launch traced here: 409 us
  waiting for transfers between devices  306 us (75%)
  matrix products  27.7 us (7%)
  local copies, waits for them, and re-layouts  26.6 us (6%)
  between operations  14.5 us (4%)
  starting transfers between devices  13.5 us (3%)
  blocking collectives  13.1 us (3%)
  other arithmetic  7.13 us (2%)
    all_to_all x1, waiting for transfers between devices, body(): lax.all_to_all(outgoing, 'row', split_axis=0, concat_axis=0, tiled=True)  94.4 us
    all_to_all x1, waiting for transfers between devices, body(): lax.all_to_all(partial_out.reshape(senders, slot_count, received_width),...  93.1 us
    ppermute x7, waiting for transfers between devices, body(): lax.ppermute(ring[-1], 'row', [(dev, (dev + 1) % 8) for dev in range(8)])  54.2 us
    all_gather x1, waiting for transfers between devices, body(): lax.all_gather(shared_up, 'row', axis=0, tiled=True)  27.7 us
    reduce_scatter x1, waiting for transfers between devices, body(): lax.psum_scatter(layer_terms.astype(jnp.bfloat16), 'col', scatter_dimensi...  19.2 us
    reduce_scatter x1, waiting for transfers between devices, body(): lax.psum_scatter(head_terms.astype(jnp.bfloat16), 'col', scatter_dimensio...  16 us
  transfers between devices with their start and end apart: 15, of which 12 were waited for; matrix products, arithmetic and copies ran while one was open for 11% of the time, Pallas kernels for 0%

profile of v1, /device:TPU:0, one launch (start us, length us, event | category | flops | bytes accessed | tf_op | source)
XLA Modules:
  0.0 408.9 jit_solution(3787224130375437808)
XLA Ops:
  9.3 3.0 collective-permute-start
  12.3 6.5 %collective-permute-done = bf16[2,128,256]{1,2,0:T(8,128)(2,1)S(1)} collective-permute-done((bf16[2,128,256]{1,2,0:T(8,128)(2,1)S(1)}, bf16[2,128,256]{1,2,0:T(8,128)(2,1)S(1)}, u32[]{:S(2)}, u32[]{:S(2)}) %collective-permute-start) | collective-permute-done | bytes 131104 | tf_op jit(solution)/shard_map/ppermute | solution.py:51
  18.8 7.7 %collective-permute-done.1 = bf16[2,128,256]{1,2,0:T(8,128)(2,1)S(1)} collective-permute-done((bf16[2,128,256]{1,2,0:T(8,128)(2,1)S(1)}, bf16[2,128,256]{1,2,0:T(8,128)(2,1)S(1)}, u32[]{:S(2)}, u32[]{:S(2)}) %collective-permute-start.1) | collective-permute-done | bytes 131104 | tf_op jit(solution)/shard_map/ppermute | solution.py:51
  27.4 6.7 %collective-permute-done.2 = bf16[2,128,256]{1,2,0:T(8,128)(2,1)S(1)} collective-permute-done((bf16[2,128,256]{1,2,0:T(8,128)(2,1)S(1)}, bf16[2,128,256]{1,2,0:T(8,128)(2,1)S(1)}, u32[]{:S(2)}, u32[]{:S(2)}) %collective-permute-start.2) | collective-permute-done | bytes 131104 | tf_op jit(solution)/shard_map/ppermute | solution.py:51
  34.8 7.7 %collective-permute-done.3 = bf16[2,128,256]{1,2,0:T(8,128)(2,1)S(1)} collective-permute-done((bf16[2,128,256]{1,2,0:T(8,128)(2,1)S(1)}, bf16[2,128,256]{1,2,0:T(8,128)(2,1)S(1)}, u32[]{:S(2)}, u32[]{:S(2)}) %collective-permute-start.3) | collective-permute-done | bytes 131104 | tf_op jit(solution)/shard_map/ppermute | solution.py:51
  42.6 8.1 %collective-permute-done.4 = bf16[2,128,256]{1,2,0:T(8,128)(2,1)S(1)} collective-permute-done((bf16[2,128,256]{1,2,0:T(8,128)(2,1)S(1)}, bf16[2,128,256]{1,2,0:T(8,128)(2,1)S(1)}, u32[]{:S(2)}, u32[]{:S(2)}) %collective-permute-start.4) | collective-permute-done | bytes 131104 | tf_op jit(solution)/shard_map/ppermute | solution.py:51
  50.7 8.8 %collective-permute-done.5 = bf16[2,128,256]{1,2,0:T(8,128)(2,1)S(1)} collective-permute-done((bf16[2,128,256]{1,2,0:T(8,128)(2,1)S(1)}, bf16[2,128,256]{1,2,0:T(8,128)(2,1)S(1)}, u32[]{:S(2)}, u32[]{:S(2)}) %collective-permute-start.5) | collective-permute-done | bytes 131104 | tf_op jit(solution)/shard_map/ppermute | solution.py:51
  59.6 8.7 %collective-permute-done.6 = bf16[2,128,256]{1,2,0:T(8,128)(2,1)S(1)} collective-permute-done((bf16[2,128,256]{1,2,0:T(8,128)(2,1)S(1)}, bf16[2,128,256]{1,2,0:T(8,128)(2,1)S(1)}, u32[]{:S(2)}, u32[]{:S(2)}) %collective-permute-start.6) | collective-permute-done | bytes 131104 | tf_op jit(solution)/shard_map/ppermute | solution.py:51
  78.5 16.0 %reduce-scatter.3.cloned.1.call-done = bf16[128,512]{1,0:T(8,128)(2,1)} async-done(((bf16[128,2048]{1,0:T(8,128)(2,1)}), bf16[128,512]{1,0:T(8,128)(2,1)}) %reduce-scatter.3.cloned.1.call-update) | async-done | bytes 131088 | tf_op jit(solution)/shard_map/reduce_scatter | solution.py:88
  95.5 5.8 %psum.7 = f32[128]{0:T(128)S(1)} all-reduce(f32[128]{0:T(128)S(1)} %fusion.41), channel_id=1, replica_groups=mesh['row'=8,'col'=4] {'col'}, use_global_device_ids=true, to_apply=%region_6.7 | all-reduce | flops 128 | bytes 1024 | tf_op jit(solution)/shard_map/psum | solution.py:94
  102.3 7.3 %all_gather.16 = bf16[128,2048]{1,0:T(8,128)(2,1)S(1)} all-gather(bf16[128,512]{1,0:T(8,128)(2,1)S(1)} %fusion.43), channel_id=1, replica_groups=mesh['row'=8,'col'=4] {'col'}, dimensions={1}, use_global_device_ids=true | all-gather | bytes 655360 | tf_op jit(solution)/shard_map/all_gather | solution.py:99
  109.7 4.2 %gather_fusion = bf16[768,2048]{1,0:T(8,128)(2,1)} fusion(bf16[129,2048]{1,0:T(8,128)(2,1)S(1)} %concatenate.10, s32[1024]{0:T(1024)S(1)} %pad_clamp_fusion.1), kind=kCustom, calls=%fused_computation | custom fusion | bytes 6294528 | tf_op jit(solution)/shard_map/gather | solution.py:131
  113.9 5.5 %all-to-all-start = ((bf16[8,96,2048]{2,1,0:T(8,128)(2,1)}), bf16[8,96,2048]{2,1,0:T(8,128)(2,1)}, u32[]{:S(2)}, u32[]{:S(2)}) async-start(bf16[8,96,2048]{2,1,0:T(8,128)(2,1)} %bitcast.109), calls=%async_computation.1 | async-start | bytes 6291456 | tf_op jit(solution)/shard_map/all_to_all | solution.py:132
  120.0 94.4 %all-to-all-done = bf16[8,96,2048]{2,1,0:T(8,128)(2,1)} async-done(((bf16[8,96,2048]{2,1,0:T(8,128)(2,1)}), bf16[8,96,2048]{2,1,0:T(8,128)(2,1)}, u32[]{:S(2)}, u32[]{:S(2)}) %all-to-all-start) | async-done | bytes 3145760 | tf_op jit(solution)/shard_map/all_to_all | solution.py:132
  214.4 4.7 %fusion.5 = f32[768,352]{0,1:T(8,128)} fusion(bf16[768,2048]{1,0:T(8,128)(2,1)} %bitcast.16, bf16[1,2048,352]{1,2,0:T(8,128)(2,1)} %param.29), kind=kOutput, calls=%fused_computation.11 | convolution fusion | flops 1107296256 | bytes 5668864 | tf_op jit(solution)/shard_map/dot_general | solution.py:135
  219.0 8.0 %convolution_convert_fusion = bf16[768,2048]{1,0:T(8,128)(2,1)} fusion(bf16[1,352,2048]{2,1,0:T(8,128)(2,1)S(1)} %copy-done, bf16[768,2048]{1,0:T(8,128)(2,1)} %bitcast.16, bf16[1,2048,352]{1,2,0:T(8,128)(2,1)} %param.30, f32[768,352]{0,1:T(8,128)} %fusion.5), kind=kOutput, calls=%fused_computation.3 | convolution fusion | flops 2217787392 | bytes 10256384 | tf_op jit(solution)/shard_map/dot_general | solution.py:138
  227.1 4.6 %all-to-all-start.1 = ((bf16[8,96,2048]{2,1,0:T(8,128)(2,1)}), bf16[8,96,2048]{2,1,0:T(8,128)(2,1)}, u32[]{:S(2)}, u32[]{:S(2)}) async-start(bf16[8,96,2048]{2,1,0:T(8,128)(2,1)} %bitcast.110), calls=%async_computation.2 | async-start | bytes 6291456 | tf_op jit(solution)/shard_map/all_to_all | solution.py:141
  233.3 3.5 fusion.63
  236.8 93.1 %all-to-all-done.1 = bf16[8,96,2048]{2,1,0:T(8,128)(2,1)} async-done(((bf16[8,96,2048]{2,1,0:T(8,128)(2,1)}), bf16[8,96,2048]{2,1,0:T(8,128)(2,1)}, u32[]{:S(2)}, u32[]{:S(2)}) %all-to-all-start.1) | async-done | bytes 3145760 | tf_op jit(solution)/shard_map/all_to_all | solution.py:141
  329.8 7.5 %gather_fusion.1 = bf16[512,2048]{1,0:T(8,128)(2,1)} fusion(bf16[768,2048]{1,0:T(8,128)(2,1)} %bitcast.21, s32[1024]{0:T(1024)S(1)} %pad_clamp_fusion), kind=kCustom, calls=%fused_computation.1 | custom fusion | bytes 4196352 | tf_op jit(solution)/shard_map/gather | solution.py:148
  340.1 4.5 %fusion.61 = (bf16[128,1,2048]{2,1,0:T(2,128)(2,1)}, bf16[128,1,2048]{2,1,0:T(2,128)(2,1)}, bf16[128,1,2048]{2,1,0:T(2,128)(2,1)}, bf16[128,1,2048]{2,1,0:T(2,128)(2,1)}) fusion(bf16[128,4,2048]{2,1,0:T(4,128)(2,1)S(1)} %reshape.220), kind=kLoop, calls=%fused_computation.122 | loop fusion | bytes 4194304 | tf_op jit(solution)/shard_map/slice | solution.py:153
  344.6 27.7 %all-gather.9.cloned.1.call-done = bf16[2048,704]{0,1:T(8,128)(2,1)} async-done(((bf16[256,704]{0,1:T(8,128)(2,1)}), bf16[2048,704]{0,1:T(8,128)(2,1)}) %all-gather.9.cloned.1.call-update) | async-done | bytes 2883600 | tf_op jit(solution)/shard_map/all_gather | solution.py:107
  372.3 8.1 %fusion.1 = bf16[128,2048]{1,0:T(8,128)(2,1)} fusion(bf16[704,2048]{1,0:T(8,128)(2,1)} %all-gather.11.cloned.1.call-done, bf16[128,2048]{1,0:T(8,128)(2,1)} %copy-done.1, bf16[2048,704]{0,1:T(8,128)(2,1)} %all-gather.9.cloned.1.call-done, bf16[128,1,2048]{2,1,0:T(2,128)(2,1)} %get-tuple-element.11, bf16[128,1,2048]{2,1,0:T(2,128)(2,1)} %get-tuple-element.9, ...), kind=kOutput, calls=%fused_computation.6 | convolution fusion | flops 742408192 | bytes 9275904 | tf_op jit(solution)/shard_map/dot_general | solution.py:111
  381.2 19.2 %reduce-scatter.5.cloned.1.call-done = bf16[128,512]{1,0:T(8,128)(2,1)} async-done(((bf16[128,2048]{1,0:T(8,128)(2,1)}), bf16[128,512]{1,0:T(8,128)(2,1)}) %reduce-scatter.5.cloned.1.call-update) | async-done | bytes 131088 | tf_op jit(solution)/shard_map/reduce_scatter | solution.py:157
  (108 shorter events, 23.1 us)
Async XLA Ops:
  7.2 211.9 %copy-start = (bf16[1,352,2048]{2,1,0:T(8,128)(2,1)S(1)}, bf16[1,352,2048]{2,1,0:T(8,128)(2,1)}, u32[]{:S(2)}) copy-start(bf16[1,352,2048]{2,1,0:T(8,128)(2,1)} %param.31) | copy-start | bytes 4325380
  7.2 63.5 %all-gather.5.cloned.1.call-start = ((), (), s32[]{:S(2)}) async-start(), calls=%async_computation.4 | async-start | bytes 1179648 | tf_op jit(solution)/shard_map/all_gather | solution.py:85
  9.3 9.6 %collective-permute-start = (bf16[2,128,256]{1,2,0:T(8,128)(2,1)S(1)}, bf16[2,128,256]{1,2,0:T(8,128)(2,1)S(1)}, u32[]{:S(2)}, u32[]{:S(2)}) collective-permute-start(bf16[2,128,256]{1,2,0:T(8,128)(2,1)S(1)} %pad_maximum_fusion), channel_id=1, source_target_pairs={{0,4},{4,8},{8,12},{12,16},{16,20},{20,24},{24,28},{28,0},{1,5},{5... | collective-permute-start | bytes 393224 | tf_op jit(solution)/shard_map/ppermute | solution.py:51
  18.8 7.7 %collective-permute-start.1 = (bf16[2,128,256]{1,2,0:T(8,128)(2,1)S(1)}, bf16[2,128,256]{1,2,0:T(8,128)(2,1)S(1)}, u32[]{:S(2)}, u32[]{:S(2)}) collective-permute-start(bf16[2,128,256]{1,2,0:T(8,128)(2,1)S(1)} %collective-permute-done), channel_id=1, source_target_pairs={{0,4},{4,8},{8,12},{12,16},{16,20},{20,24},{24,28},{28,0},{1,5},{5... | collective-permute-start | bytes 393224 | tf_op jit(solution)/shard_map/ppermute | solution.py:51
  26.5 7.7 %collective-permute-start.2 = (bf16[2,128,256]{1,2,0:T(8,128)(2,1)S(1)}, bf16[2,128,256]{1,2,0:T(8,128)(2,1)S(1)}, u32[]{:S(2)}, u32[]{:S(2)}) collective-permute-start(bf16[2,128,256]{1,2,0:T(8,128)(2,1)S(1)} %collective-permute-done.1), channel_id=1, source_target_pairs={{0,4},{4,8},{8,12},{12,16},{16,20},{20,24},{24,28},{28,0},{1,5},{5... | collective-permute-start | bytes 393224 | tf_op jit(solution)/shard_map/ppermute | solution.py:51
  26.5 68.0 %reduce-scatter.3.cloned.1.call-start = ((), (), s32[]{:S(2)}) async-start(), calls=%async_computation.5 | async-start | bytes 655360 | tf_op jit(solution)/shard_map/reduce_scatter | solution.py:88
  34.2 8.3 %collective-permute-start.3 = (bf16[2,128,256]{1,2,0:T(8,128)(2,1)S(1)}, bf16[2,128,256]{1,2,0:T(8,128)(2,1)S(1)}, u32[]{:S(2)}, u32[]{:S(2)}) collective-permute-start(bf16[2,128,256]{1,2,0:T(8,128)(2,1)S(1)} %collective-permute-done.2), channel_id=1, source_target_pairs={{0,4},{4,8},{8,12},{12,16},{16,20},{20,24},{24,28},{28,0},{1,5},{5... | collective-permute-start | bytes 393224 | tf_op jit(solution)/shard_map/ppermute | solution.py:51
  42.5 8.2 %collective-permute-start.4 = (bf16[2,128,256]{1,2,0:T(8,128)(2,1)S(1)}, bf16[2,128,256]{1,2,0:T(8,128)(2,1)S(1)}, u32[]{:S(2)}, u32[]{:S(2)}) collective-permute-start(bf16[2,128,256]{1,2,0:T(8,128)(2,1)S(1)} %collective-permute-done.3), channel_id=1, source_target_pairs={{0,4},{4,8},{8,12},{12,16},{16,20},{20,24},{24,28},{28,0},{1,5},{5... | collective-permute-start | bytes 393224 | tf_op jit(solution)/shard_map/ppermute | solution.py:51
  50.7 8.8 %collective-permute-start.5 = (bf16[2,128,256]{1,2,0:T(8,128)(2,1)S(1)}, bf16[2,128,256]{1,2,0:T(8,128)(2,1)S(1)}, u32[]{:S(2)}, u32[]{:S(2)}) collective-permute-start(bf16[2,128,256]{1,2,0:T(8,128)(2,1)S(1)} %collective-permute-done.4), channel_id=1, source_target_pairs={{0,4},{4,8},{8,12},{12,16},{16,20},{20,24},{24,28},{28,0},{1,5},{5... | collective-permute-start | bytes 393224 | tf_op jit(solution)/shard_map/ppermute | solution.py:51
  59.5 8.8 %collective-permute-start.6 = (bf16[2,128,256]{1,2,0:T(8,128)(2,1)S(1)}, bf16[2,128,256]{1,2,0:T(8,128)(2,1)S(1)}, u32[]{:S(2)}, u32[]{:S(2)}) collective-permute-start(bf16[2,128,256]{1,2,0:T(8,128)(2,1)S(1)} %collective-permute-done.5), channel_id=1, source_target_pairs={{0,4},{4,8},{8,12},{12,16},{16,20},{20,24},{24,28},{28,0},{1,5},{5... | collective-permute-start | bytes 393224 | tf_op jit(solution)/shard_map/ppermute | solution.py:51
  70.2 4.0 copy-start.12
  70.7 23.9 %copy-start.2 = (bf16[128,512]{1,0:T(8,128)(2,1)S(1)}, bf16[128,512]{1,0:T(8,128)(2,1)}, u32[]{:S(2)}) copy-start(bf16[128,512]{1,0:T(8,128)(2,1)} %param.22) | copy-start | bytes 393220
  73.2 160.1 %all-gather.7.cloned.1.call-start = ((), (), s32[]{:S(2)}) async-start(), calls=%async_computation.6 | async-start | bytes 3244032 | tf_op jit(solution)/shard_map/all_gather | solution.py:102
  109.6 123.7 %copy-start.1 = (bf16[128,2048]{1,0:T(8,128)(2,1)}, bf16[128,2048]{1,0:T(8,128)(2,1)S(1)}, u32[]{:S(2)}) copy-start(bf16[128,2048]{1,0:T(8,128)(2,1)S(1)} %all_gather.16) | copy-start | bytes 1572868
  113.9 100.5 %all-to-all-start = ((bf16[8,96,2048]{2,1,0:T(8,128)(2,1)}), bf16[8,96,2048]{2,1,0:T(8,128)(2,1)}, u32[]{:S(2)}, u32[]{:S(2)}) async-start(bf16[8,96,2048]{2,1,0:T(8,128)(2,1)} %bitcast.109), calls=%async_computation.1 | async-start | bytes 6291456 | tf_op jit(solution)/shard_map/all_to_all | solution.py:132
  119.4 225.2 %all-gather.11.cloned.1.call-start = ((), (), s32[]{:S(2)}) async-start(), calls=%async_computation.8 | async-start | bytes 3244032 | tf_op jit(solution)/shard_map/all_gather | solution.py:113
  227.0 5.4 %copy-start.9 = (bf16[2048]{0:T(1024)(128)(2,1)S(1)}, bf16[2048]{0:T(1024)(128)(2,1)}, u32[]{:S(2)}) copy-start(bf16[2048]{0:T(1024)(128)(2,1)} %param.28) | copy-start | bytes 12292
  227.1 5.4 %copy-start.11 = (f32[128,4]{0,1:T(4,128)S(1)}, f32[128,4]{0,1:T(4,128)}, u32[]{:S(2)}) copy-start(f32[128,4]{0,1:T(4,128)} %param.33) | copy-start | bytes 6148
  227.1 102.8 %all-to-all-start.1 = ((bf16[8,96,2048]{2,1,0:T(8,128)(2,1)}), bf16[8,96,2048]{2,1,0:T(8,128)(2,1)}, u32[]{:S(2)}, u32[]{:S(2)}) async-start(bf16[8,96,2048]{2,1,0:T(8,128)(2,1)} %bitcast.110), calls=%async_computation.2 | async-start | bytes 6291456 | tf_op jit(solution)/shard_map/all_to_all | solution.py:141
  231.6 140.7 %all-gather.9.cloned.1.call-start = ((), (), s32[]{:S(2)}) async-start(), calls=%async_computation.7 | async-start | bytes 3244032 | tf_op jit(solution)/shard_map/all_gather | solution.py:107
  232.2 168.2 %reduce-scatter.5.cloned.1.call-start = ((), (), s32[]{:S(2)}) async-start(), calls=%async_computation.9 | async-start | bytes 655360 | tf_op jit(solution)/shard_map/reduce_scatter | solution.py:157
  372.3 8.1 %copy-start.6 = (bf16[128,2,128]{0,2,1:T(8,128)(2,1)S(1)}, bf16[128,2,128]{0,2,1:T(8,128)(2,1)}, u32[]{:S(2)}) copy-start(bf16[128,2,128]{0,2,1:T(8,128)(2,1)} %copy-done.5) | copy-start | bytes 196612
  372.3 28.1 %copy-start.3 = (bf16[128,512]{1,0:T(8,128)(2,1)S(1)}, bf16[128,512]{1,0:T(8,128)(2,1)}, u32[]{:S(2)}) copy-start(bf16[128,512]{1,0:T(8,128)(2,1)} %param.22) | copy-start | bytes 393220
  372.3 28.1 %copy-start.4 = (bf16[128,512]{1,0:T(8,128)(2,1)S(1)}, bf16[128,512]{1,0:T(8,128)(2,1)}, u32[]{:S(2)}) copy-start(bf16[128,512]{1,0:T(8,128)(2,1)} %reduce-scatter.3.cloned.1.call-done) | copy-start | bytes 393220
  (4 other events, 7.9 us)
Sparse Core Ops, SparseCore 0:
  26.6 43.2 all-gather.4
  73.3 21.1 reduce-scatter.2
  96.8 109.6 all-gather.6
  208.5 102.8 all-gather.10
  313.5 58.7 all-gather.8
  380.6 19.8 reduce-scatter.4
